TPU v7x, 32 devices: a whole 2x2x4 slice. The times are simulated.
32 devices in a mesh: dp: 2 (over x), space: 16 (over z, y, core).
Axes of the slice: x: 2, y: 2, z: 4, core: 2. Of those that a mesh axis runs over, the one named last changes fastest.
Arguments:
- tiles_in: bfloat16 [2, 64, 8, 8, 384], P('dp', 'space'), may hold values from -6 to 6
- upstream: bfloat16 [2, 64, 8, 8, 384], P('dp', 'space'), may hold values from -1.1953125 to 1.1953125
- pool_weight: float32 [2, 64], P('dp', 'space'), may hold values from 0.25 to 4
- slide_cot: float32 [2, 384], P('dp'), may hold values from -6 to 6
- adjacency: int32 [2, 64, 8], P('dp', 'space'), may hold values from -1 to 63, as said below
- counts: int32 [2, 16], P('dp', 'space'), may hold values from 1 to 4, as said below
- kernel: float32 [7, 7, 384], replicated, may hold values from -0.875 to 0.875
- norm_gain: float32 [384], replicated, may hold values from 0.5 to 1.5
- w_in: bfloat16 [384, 1536], replicated, may hold values from -0.3125 to 0.3125
- w_out: bfloat16 [1536, 384], replicated, may hold values from -0.15625 to 0.15625
- layer_scale: float32 [384], replicated, may hold values from 0.1 to 1
Outputs:
- embedding: float32 [2, 384], P('dp')
- grad_tiles: bfloat16 [2, 64, 8, 8, 384], P('dp', 'space')
- grad_w_out: float32 [1536, 384], P('space')
- grad_kernel: float32 [7, 7, 384], replicated
Inputs may be any that keep to these rules, and one draw needn't show every extreme that they name: Slots form blocks of 4; block k of a slide is one row of tiles, its live tiles in its first counts slots in column order; the last block of every slide is full, and often another one too. `adjacency`: tiles lie on a grid: entries 0, 4, 5 name live slots of the block before the tile's own, entries 1, 6, 7 of the block after it, entries 2 and 3 of its own block. The lists are mutual (b is the north neighbour of a exactly when a is the south neighbour of b, and likewise for the other directions). Slots that are not live have no neighbours and are named by none.
All inputs are finite; a program needn't handle non-finite values.
Results may differ from a plain program's by a relative error of at most 0.011.
Values may be sent and summed in bfloat16 or wider, within the bound.
No kernel may reach another device: no remote copies, remote signals or barrier semaphores. Data moves between devices by JAX's collectives and lax.ppermute only.
A program may use at most 64 MiB of HBM per device.

v0:
```python
import jax
import jax.numpy as jnp
from jax import lax
from jax.sharding import PartitionSpec as P

sqrt_half = 0.7071067811865476
inv_root_two_pi = 0.3989422804014327


def passed_along(value, axis, steps):
    count = lax.axis_size(axis)
    leading, last = (max(0, -steps), min(count, count - steps))
    return lax.ppermute(value, axis, [(source, source + steps) for source in range(leading, last)])


def depthwise(padded, kernel, tile_side):
    total = jnp.zeros(padded.shape[:1] + (tile_side, tile_side, padded.shape[3]), jnp.float32)
    for row_tap in range(7):
        for col_tap in range(7):
            window = padded[
                :, row_tap : row_tap + tile_side, col_tap : col_tap + tile_side, :
            ].astype(jnp.float32)
            total = total + window * kernel[row_tap, col_tap]
    return total


def pick(source, wanted, offset):
    valid = wanted >= 0
    index = jnp.clip(wanted - offset, 0, source.shape[0] - 1)
    chosen = jnp.take(source, index, axis=0)
    return jnp.where(valid[:, None, None, None], chosen, jnp.zeros_like(chosen))


def frame(
    own, north_rows, south_rows, right_cols, left_cols, wanted, north_base, own_base, south_base
):
    tile_side = own.shape[1]
    upper = jnp.concatenate(
        [
            pick(north_rows, wanted[:, 4], north_base)[:, :, tile_side - 3 :],
            pick(north_rows, wanted[:, 0], north_base),
            pick(north_rows, wanted[:, 5], north_base)[:, :, :3],
        ],
        axis=2,
    )
    middle = jnp.concatenate(
        [pick(right_cols, wanted[:, 2], own_base), own, pick(left_cols, wanted[:, 3], own_base)],
        axis=2,
    )
    lower = jnp.concatenate(
        [
            pick(south_rows, wanted[:, 6], south_base)[:, :, tile_side - 3 :],
            pick(south_rows, wanted[:, 1], south_base),
            pick(south_rows, wanted[:, 7], south_base)[:, :, :3],
        ],
        axis=2,
    )
    return jnp.concatenate([upper, middle, lower], axis=1)


def block_pass(
    padded, own, upstream, pool_weight, live, slide_cot, kernel, norm_gain, w_in, w_out, layer_scale
):
    tile_side = own.shape[1]
    channels = own.shape[3]
    conv_out = depthwise(padded, kernel, tile_side)
    centred = conv_out - jnp.mean(conv_out, axis=-1, keepdims=True)
    inv_std = lax.rsqrt(jnp.mean(centred * centred, axis=-1, keepdims=True) + 1e-06)
    normed = centred * inv_std
    lifted = (normed * norm_gain).astype(jnp.bfloat16).reshape(-1, channels)
    pre = jnp.dot(lifted, w_in, preferred_element_type=jnp.float32)
    cdf = 0.5 * (1.0 + jax.scipy.special.erf(pre * sqrt_half))
    activated = (pre * cdf).astype(jnp.bfloat16)
    mixed = jnp.dot(activated, w_out, preferred_element_type=jnp.float32).reshape(own.shape)
    block_out = own.astype(jnp.float32) + layer_scale * mixed
    weight_live = live * pool_weight
    emb_term = jnp.sum(weight_live[:, None] * jnp.sum(block_out, axis=(1, 2)), axis=0) / tile_side
    extra = pool_weight[:, None] * slide_cot[None, :] / tile_side
    grad_out = live[:, None, None, None] * (upstream.astype(jnp.float32) + extra[:, None, None, :])
    grad_mixed = (grad_out * layer_scale).astype(jnp.bfloat16).reshape(-1, channels)
    grad_act = lax.dot_general(
        grad_mixed, w_out, (((1,), (1,)), ((), ())), preferred_element_type=jnp.float32
    )
    density = jnp.exp(-0.5 * pre * pre) * inv_root_two_pi
    grad_pre = (grad_act * (cdf + pre * density)).astype(jnp.bfloat16)
    grad_lift = lax.dot_general(
        grad_pre, w_in, (((1,), (1,)), ((), ())), preferred_element_type=jnp.float32
    )
    grad_normed = grad_lift.reshape(own.shape) * norm_gain
    grad_conv = inv_std * (
        grad_normed
        - jnp.mean(grad_normed, axis=-1, keepdims=True)
        - normed * jnp.mean(grad_normed * normed, axis=-1, keepdims=True)
    )
    kernel_rows = []
    for row_tap in range(7):
        for col_tap in range(7):
            window = padded[
                :, row_tap : row_tap + tile_side, col_tap : col_tap + tile_side, :
            ].astype(jnp.float32)
            kernel_rows.append(jnp.sum(window * grad_conv, axis=(0, 1, 2)))
    kernel_grad = jnp.stack(kernel_rows).reshape(7, 7, channels)
    return (emb_term, grad_out, grad_conv, activated, grad_mixed, kernel_grad)


def per_device(
    tiles_in,
    upstream,
    pool_weight,
    slide_cot,
    adjacency,
    counts,
    kernel,
    norm_gain,
    w_in,
    w_out,
    layer_scale,
):
    own = tiles_in[0]
    capacity = own.shape[0]
    tile_side = own.shape[1]
    position = lax.axis_index("space")
    own_base = position * capacity
    north_base = own_base - capacity
    south_base = own_base + capacity
    wanted = adjacency[0]
    live = (jnp.arange(capacity, dtype=jnp.int32) < counts[0, 0]).astype(jnp.float32)
    north_rows = passed_along(own[:, tile_side - 3 :], "space", 1)
    south_rows = passed_along(own[:, :3], "space", -1)
    padded = frame(
        own,
        north_rows,
        south_rows,
        own[:, :, tile_side - 3 :],
        own[:, :, :3],
        wanted,
        north_base,
        own_base,
        south_base,
    )
    emb_term, grad_out, grad_conv, activated, grad_mixed, kernel_grad = block_pass(
        padded,
        own,
        upstream[0],
        pool_weight[0],
        live,
        slide_cot[0],
        kernel,
        norm_gain,
        w_in,
        w_out,
        layer_scale,
    )
    embedding = lax.psum(emb_term, "space")
    local_weight = lax.dot_general(
        activated, grad_mixed, (((0,), (0,)), ((), ())), preferred_element_type=jnp.float32
    )
    whole_weight, kernel_dp = (
        lax.psum(local_weight.astype(jnp.bfloat16), "dp").astype(jnp.float32),
        lax.psum(kernel_grad.astype(jnp.bfloat16), "dp").astype(jnp.float32),
    )
    weight_share = lax.psum_scatter(whole_weight, "space", scatter_dimension=0, tiled=True)
    kernel_total = lax.psum(kernel_dp, "space")
    grad_north = passed_along(
        grad_conv[:, tile_side - 3 :].astype(jnp.bfloat16), "space", 1
    ).astype(jnp.float32)
    grad_south = passed_along(grad_conv[:, :3].astype(jnp.bfloat16), "space", -1).astype(
        jnp.float32
    )
    padded_grad = frame(
        grad_conv,
        grad_north,
        grad_south,
        grad_conv[:, :, tile_side - 3 :],
        grad_conv[:, :, :3],
        wanted,
        north_base,
        own_base,
        south_base,
    )
    back = depthwise(padded_grad, kernel[::-1, ::-1], tile_side)
    grad_tiles = ((grad_out + back) * live[:, None, None, None]).astype(jnp.bfloat16)
    return (embedding[None, :], grad_tiles[None], weight_share, kernel_total)


def solution(mesh):
    return jax.shard_map(
        per_device,
        mesh=mesh,
        in_specs=(
            P("dp", "space", None, None, None),
            P("dp", "space", None, None, None),
            P("dp", "space"),
            P("dp", None),
            P("dp", "space", None),
            P("dp", "space"),
            P(),
            P(),
            P(),
            P(),
            P(),
        ),
        out_specs=(P("dp", None), P("dp", "space", None, None, None), P("space", None), P()),
        check_vma=False,
    )
```

profile of v0, /device:TPU:0, one launch (start us, length us, event | category | flops | bytes accessed | tf_op | source)
XLA Modules:
  0.0 189.6 jit_solution(16808455452502542343)
XLA Ops:
  7.2 1.0 fusion.191
  8.3 2.4 %collective-permute-start = (bf16[4,3,8,384]{3,2,1,0:T(8,128)(2,1)S(1)}, bf16[4,3,8,384]{3,2,1,0:T(8,128)(2,1)S(1)}, u32[]{:S(2)}, u32[]{:S(2)}) collective-permute-start(bf16[4,3,8,384]{3,2,1,0:T(8,128)(2,1)S(1)} %get-tuple-element.146), channel_id=1, source_target_pairs={{0,1},{1,2},{2,3},{3,4},{4,5},{5,6},{6,7},{7,8},{8,9},{9,10},{10,1... | collective-permute-start | bytes 221192 | tf_op jit(solution)/shard_map/ppermute | solution.py:13
  10.7 1.3 collective-permute-start.1
  12.0 1.1 fusion.192
  13.1 1.3 compare_reduce_fusion.7
  14.5 1.3 clamp_reduce_fusion.7
  15.9 0.6 compare_and_fusion.4
  16.5 0.6 compare_and_fusion.2
  17.1 1.0 slice_reduce_fusion.46
  18.1 1.9 %slice_reduce_fusion.48 = (f32[384]{0:T(512)S(1)}, f32[384]{0:T(512)S(1)}, f32[384]{0:T(512)S(1)}, f32[384]{0:T(512)S(1)}, f32[384]{0:T(512)S(1)}, /*index=5*/f3...) fusion(f32[7,7,384]{2,1,0:T(8,128)} %param.25), kind=kLoop, calls=%fused_computation.487 | loop fusion | bytes 58368 | tf_op jit(solution)/shard_map/slice | solution.py:23
  20.1 1.9 slice_reduce_fusion.47
  23.0 0.7 reduce.66
  23.7 1.2 compare_select_fusion.8
  24.8 0.7 multiply_multiply_fusion.1
  25.6 0.6 gather_fusion.4
  26.2 0.6 gather_fusion.3
  26.9 0.8 select_select_fusion.4
  27.7 0.8 select_select_fusion.5
  28.5 0.8 fusion.169
  29.3 0.6 gather_fusion.2
  29.9 0.8 fusion.182
  30.7 0.6 gather_fusion.1
  31.3 0.6 gather_fusion
  32.0 0.6 gather_fusion.7
  32.8 0.6 gather_fusion.6
  33.5 0.6 gather_fusion.5
  34.1 0.8 fusion.181
  34.9 0.4 maximum_maximum_fusion.2
  35.5 4.3 %fusion.187 = (f32[4,8,8]{2,1,0:T(8,128)S(1)}, f32[4,8,8,384]{3,2,1,0:T(8,128)S(1)}) fusion(f32[384]{0:T(512)S(1)} %get-tuple-element.114, bf16[4,11,14,384]{3,2,1,0:T(8,128)(2,1)S(1)} %get-tuple-element.143, f32[384]{0:T(512)S(1)} %get-tuple-element.115, f32[384]{0:T(512)S(1)} %get-tuple-element.68, f32[384]{0:T(512)S(1)} %get-tuple-element.69, ...), kind=kLoop, calls=%fused_computation.495 | loop fusion | flops 16219904 | bytes 9071104 | tf_op jit(solution)/shard_map/reduce_sum | solution.py:67
  39.8 0.2 multiply_reduce_fusion.2
  40.1 0.1 multiply_convert_fusion.1
  40.2 2.0 %multiply_convert_fusion = (bf16[256,1536]{1,0:T(8,128)(2,1)}, f32[256,1536]{1,0:T(8,128)}) fusion(bf16[256,384]{1,0:T(8,128)(2,1)S(1)} %bitcast.50, bf16[384,1536]{1,0:T(8,128)(2,1)S(1)} %copy-done), kind=kOutput, calls=%fused_computation.24 | convolution fusion | flops 303955968 | bytes 3735552 | tf_op jit(solution)/shard_map/dot_general | solution.py:71
  42.2 3.1 %multiply_reduce_fusion.1 = (f32[256]{0:T(256)S(1)}, f32[256,384]{1,0:T(8,128)S(1)}) fusion(f32[384]{0:T(512)S(1)} %copy-done.7, bf16[384,1536]{1,0:T(8,128)(2,1)S(1)} %copy-done, bf16[256,384]{1,0:T(8,128)(2,1)} %fusion.169, bf16[1536,384]{1,0:T(8,128)(2,1)} %param.28, f32[256,1536]{1,0:T(8,128)} %get-tuple-element.153), kind=kOutput, calls=%fused_computation.359 | convolution fusion | flops 608108288 | bytes 4524544 | tf_op jit(solution)/shard_map/dot_general | solution.py:86
  45.3 0.2 multiply_reduce_fusion
  45.7 2.8 %convolution_convert_fusion = bf16[1536,384]{1,0:T(8,128)(2,1)} fusion(bf16[256,1536]{1,0:T(8,128)(2,1)} %get-tuple-element.152, bf16[256,384]{1,0:T(8,128)(2,1)} %fusion.169), kind=kOutput, calls=%fused_computation.16 | convolution fusion | flops 302579712 | bytes 2162688 | tf_op jit(solution)/shard_map/dot_general | solution.py:155
  48.6 2.0 %fusion.186 = (bf16[4,8,8,384]{3,2,1,0:T(8,128)(2,1)}, f32[4,8,8,384]{3,2,1,0:T(8,128)S(1)}) fusion(f32[4,8,8]{2,1,0:T(8,128)S(1)} %broadcast_multiply_fusion, f32[4,8,8,384]{3,2,1,0:T(8,128)S(1)} %get-tuple-element.137, f32[4,8,8]{2,1,0:T(8,128)S(1)} %broadcast_multiply_fusion.1, f32[4,8,8]{2,1,0:T(8,128)S(1)} %div.33, f32[384]{0:T(512)S(1)} %copy-done.7, ...), kind=kLoop, calls=%fused_computation.494 | loop fusion | flops 786432 | bytes 1381888 | tf_op jit(solution)/shard_map/convert.101
  50.5 3.1 %fusion.85 = (bf16[384]{0:T(512)(128)(2,1)}, bf16[384]{0:T(512)(128)(2,1)}, bf16[384]{0:T(512)(128)(2,1)}, bf16[384]{0:T(512)(128)(2,1)}, bf16[384]{0:T(512)(128...) fusion(f32[4,8,8,384]{3,2,1,0:T(8,128)S(1)} %get-tuple-element., ...), kind=kOutput, calls=%fused_computation.225 | convolution fusion | flops 306998016 | bytes 3505152 | tf_op jit(solution)/shard_map/dot_general | solution.py:74
  53.7 0.9 gather_fusion.12
  54.6 0.8 gather_fusion.11
  55.4 0.6 fusion.190
  56.1 5.1 %collective-permute-start.2 = (bf16[4,3,8,384]{3,2,1,0:T(8,128)(2,1)}, bf16[4,3,8,384]{3,2,1,0:T(8,128)(2,1)S(1)}, u32[]{:S(2)}, u32[]{:S(2)}) collective-permute-start(bf16[4,3,8,384]{3,2,1,0:T(8,128)(2,1)} %get-tuple-element.144), channel_id=1, source_target_pairs={{0,1},{1,2},{2,3},{3,4},{4,5},{5,6},{6,7},{7,8},{8,9},{9,10},{10,1... | collective-permute-start | bytes 221192 | tf_op jit(solution)/shard_map/ppermute | solution.py:13
  61.2 1.5 collective-permute-start.3
  62.7 0.7 multiply_reduce_fusion.3
  63.4 0.8 select_select_fusion
  64.2 0.8 select_select_fusion.1
  65.0 31.3 %all-reduce.4.cloned.1.call-done = bf16[1536,384]{1,0:T(8,128)(2,1)} async-done(((bf16[1536,384]{1,0:T(8,128)(2,1)}), bf16[1536,384]{1,0:T(8,128)(2,1)}) %all-reduce.4.cloned.1.call-update) | async-done | bytes 1179664 | tf_op jit(solution)/shard_map/psum | solution.py:159
  96.2 2.8 %convert_element_type.315 = f32[1536,384]{1,0:T(8,128)} convert(bf16[1536,384]{1,0:T(8,128)(2,1)} %all-reduce.4.cloned.1.call-done) | non-fusion elementwise | flops 589824 | bytes 3538944 | tf_op jit(solution)/shard_map/convert_element_type | solution.py:159
  99.1 1.0 fusion.53
  100.2 1.0 fusion.103
  101.2 0.2 fusion.35
  102.0 0.3 stack.249
  102.3 7.4 %psum.30 = bf16[7,7,384]{2,1,0:T(8,128)(2,1)S(1)} all-reduce(bf16[7,7,384]{2,1,0:T(8,128)(2,1)S(1)} %convert_element_type.316), channel_id=1, replica_groups=mesh['dp'=2,'space'=16] {'dp'}, use_global_device_ids=true, to_apply=%region_58.63 | all-reduce | flops 18816 | bytes 75264 | tf_op jit(solution)/shard_map/psum | solution.py:160
  109.8 61.0 %all-reduce.5 = (f32[1,384]{1,0:T(1,128)}, f32[7,7,384]{2,1,0:T(8,128)}) all-reduce(f32[1,384]{1,0:T(1,128)S(1)} %broadcast_in_dim.154, bf16[7,7,384]{2,1,0:T(8,128)(2,1)S(1)} %psum.30), channel_id=1, replica_groups=mesh['dp'=2,'space'=16] {'space'}, use_global_device_ids=true, to_apply=%region_4.7 | all-reduce | flops 19200 | bytes 115968 | tf_op jit(solution)/shard_map/psum | solution.py:154
  170.9 0.7 gather_fusion.10
  171.6 0.7 gather_fusion.9
  172.3 0.7 gather_fusion.8
  173.0 0.7 gather_fusion.15
  173.7 0.7 gather_fusion.14
  174.4 0.7 gather_fusion.13
  175.1 0.8 fusion.178
  176.1 0.8 fusion.177
  177.4 0.3 maximum_maximum_fusion
  177.7 0.3 copy-done.5
  178.3 4.4 %fusion.175 = bf16[1,4,8,8,384]{4,3,2,1,0:T(8,128)(2,1)} fusion(f32[384]{0:T(512)S(1)} %copy-done.19, f32[4,11,14,384]{3,2,1,0:T(8,128)S(1)} %get-tuple-element.139, f32[384]{0:T(512)S(1)} %copy-done.54, f32[384]{0:T(512)S(1)} %get-tuple-element.105, f32[384]{0:T(512)S(1)} %copy-done.13, f32[384]{0:T(512)S(1)} %copy-done.11, f32[384]{0:T(512)S(1)} %copy-done.9, ...), kind=kLoop, calls=%fused_computation.371 | loop fusion | flops 10715136 | bytes 17677840 | tf_op jit(solution)/shard_map/broadcast_in_dim | solution.py:183
  (318 shorter events, 2.0 us)
Async XLA Ops:
  7.2 33.0 %copy-start = (bf16[384,1536]{1,0:T(8,128)(2,1)S(1)}, bf16[384,1536]{1,0:T(8,128)(2,1)}, u32[]{:S(2)}) copy-start(bf16[384,1536]{1,0:T(8,128)(2,1)} %param.27) | copy-start | bytes 3538948
  7.2 21.3 %copy-start.69 = (f32[384]{0:T(512)S(1)}, f32[384]{0:T(512)}, u32[]{:S(2)}) copy-start(f32[384]{0:T(512)} %param.29) | copy-start | bytes 4612
  7.2 21.3 %copy-start.4 = (bf16[1,4,8,8,384]{4,3,2,1,0:T(8,128)(2,1)S(1)}, bf16[1,4,8,8,384]{4,3,2,1,0:T(8,128)(2,1)}, u32[]{:S(2)}) copy-start(bf16[1,4,8,8,384]{4,3,2,1,0:T(8,128)(2,1)} %param.20) | copy-start | bytes 589828
  7.2 89.0 %all-reduce.4.cloned.1.call-start = ((), (), s32[]{:S(2)}) async-start(), calls=%async_computation.1 | async-start | bytes 2359296 | tf_op jit(solution)/shard_map/psum | solution.py:159
  8.3 21.0 %collective-permute-start = (bf16[4,3,8,384]{3,2,1,0:T(8,128)(2,1)S(1)}, bf16[4,3,8,384]{3,2,1,0:T(8,128)(2,1)S(1)}, u32[]{:S(2)}, u32[]{:S(2)}) collective-permute-start(bf16[4,3,8,384]{3,2,1,0:T(8,128)(2,1)S(1)} %get-tuple-element.146), channel_id=1, source_target_pairs={{0,1},{1,2},{2,3},{3,4},{4,5},{5,6},{6,7},{7,8},{8,9},{9,10},{10,1... | collective-permute-start | bytes 221192 | tf_op jit(solution)/shard_map/ppermute | solution.py:13
  10.7 21.3 %collective-permute-start.1 = (bf16[4,3,8,384]{3,2,1,0:T(8,128)(2,1)S(1)}, bf16[4,3,8,384]{3,2,1,0:T(8,128)(2,1)S(1)}, u32[]{:S(2)}, u32[]{:S(2)}) collective-permute-start(bf16[4,3,8,384]{3,2,1,0:T(8,128)(2,1)S(1)} %get-tuple-element.147), channel_id=1, source_target_pairs={{1,0},{2,1},{3,2},{4,3},{5,4},{6,5},{7,6},{8,7},{9,8},{10,9},{11,1... | collective-permute-start | bytes 221192 | tf_op jit(solution)/shard_map/ppermute | solution.py:13
  14.4 18.2 %copy-start.81 = (pred[4]{0:T(512)(128)(4,1)}, pred[4]{0:T(512)(128)(4,1)S(1)}, u32[]{:S(2)}) copy-start(pred[4]{0:T(512)(128)(4,1)S(1)} %get-tuple-element.123) | copy-start | bytes 16
  14.4 18.2 %copy-start.87 = (pred[4]{0:T(512)(128)(4,1)}, pred[4]{0:T(512)(128)(4,1)S(1)}, u32[]{:S(2)}) copy-start(pred[4]{0:T(512)(128)(4,1)S(1)} %get-tuple-element.116) | copy-start | bytes 16
  14.4 18.2 %copy-start.89 = (pred[4]{0:T(512)(128)(4,1)}, pred[4]{0:T(512)(128)(4,1)S(1)}, u32[]{:S(2)}) copy-start(pred[4]{0:T(512)(128)(4,1)S(1)} %get-tuple-element.122) | copy-start | bytes 16
  14.4 18.2 %copy-start.91 = (pred[4]{0:T(512)(128)(4,1)}, pred[4]{0:T(512)(128)(4,1)S(1)}, u32[]{:S(2)}) copy-start(pred[4]{0:T(512)(128)(4,1)S(1)} %get-tuple-element.121) | copy-start | bytes 16
  14.5 18.2 %copy-start.92 = (pred[4]{0:T(512)(128)(4,1)}, pred[4]{0:T(512)(128)(4,1)S(1)}, u32[]{:S(2)}) copy-start(pred[4]{0:T(512)(128)(4,1)S(1)} %get-tuple-element.120) | copy-start | bytes 16
  14.5 18.2 %copy-start.85 = (pred[4]{0:T(512)(128)(4,1)}, pred[4]{0:T(512)(128)(4,1)S(1)}, u32[]{:S(2)}) copy-start(pred[4]{0:T(512)(128)(4,1)S(1)} %get-tuple-element.117) | copy-start | bytes 16
  14.5 18.9 %copy-start.79 = (pred[4]{0:T(512)(128)(4,1)}, pred[4]{0:T(512)(128)(4,1)S(1)}, u32[]{:S(2)}) copy-start(pred[4]{0:T(512)(128)(4,1)S(1)} %get-tuple-element.118) | copy-start | bytes 16
  14.5 19.6 %copy-start.83 = (pred[4]{0:T(512)(128)(4,1)}, pred[4]{0:T(512)(128)(4,1)S(1)}, u32[]{:S(2)}) copy-start(pred[4]{0:T(512)(128)(4,1)S(1)} %get-tuple-element.119) | copy-start | bytes 16
  15.8 16.9 %copy-start.97 = (pred[4]{0:T(512)(128)(4,1)}, pred[4]{0:T(512)(128)(4,1)S(1)}, u32[]{:S(2)}) copy-start(pred[4]{0:T(512)(128)(4,1)S(1)} %get-tuple-element.160) | copy-start | bytes 16
  15.8 17.6 %copy-start.93 = (pred[4]{0:T(512)(128)(4,1)}, pred[4]{0:T(512)(128)(4,1)S(1)}, u32[]{:S(2)}) copy-start(pred[4]{0:T(512)(128)(4,1)S(1)} %get-tuple-element.161) | copy-start | bytes 16
  15.9 16.8 %copy-start.95 = (pred[4]{0:T(512)(128)(4,1)}, pred[4]{0:T(512)(128)(4,1)S(1)}, u32[]{:S(2)}) copy-start(pred[4]{0:T(512)(128)(4,1)S(1)} %get-tuple-element.166) | copy-start | bytes 16
  15.9 16.8 %copy-start.99 = (pred[4]{0:T(512)(128)(4,1)}, pred[4]{0:T(512)(128)(4,1)S(1)}, u32[]{:S(2)}) copy-start(pred[4]{0:T(512)(128)(4,1)S(1)} %get-tuple-element.167) | copy-start | bytes 16
  18.0 17.3 %copy-start.8 = (f32[384]{0:T(512)}, f32[384]{0:T(512)S(1)}, u32[]{:S(2)}) copy-start(f32[384]{0:T(512)S(1)} %get-tuple-element.111) | copy-start | bytes 4612
  18.0 17.3 %copy-start.10 = (f32[384]{0:T(512)}, f32[384]{0:T(512)S(1)}, u32[]{:S(2)}) copy-start(f32[384]{0:T(512)S(1)} %get-tuple-element.112) | copy-start | bytes 4612
  18.1 17.3 %copy-start.12 = (f32[384]{0:T(512)}, f32[384]{0:T(512)S(1)}, u32[]{:S(2)}) copy-start(f32[384]{0:T(512)S(1)} %get-tuple-element.113) | copy-start | bytes 4612
  18.1 17.3 %copy-start.14 = (f32[384]{0:T(512)}, f32[384]{0:T(512)S(1)}, u32[]{:S(2)}) copy-start(f32[384]{0:T(512)S(1)} %get-tuple-element.114) | copy-start | bytes 4612
  18.1 17.3 %copy-start.16 = (f32[384]{0:T(512)}, f32[384]{0:T(512)S(1)}, u32[]{:S(2)}) copy-start(f32[384]{0:T(512)S(1)} %get-tuple-element.115) | copy-start | bytes 4612
  20.0 15.4 %copy-start.18 = (f32[384]{0:T(512)}, f32[384]{0:T(512)S(1)}, u32[]{:S(2)}) copy-start(f32[384]{0:T(512)S(1)} %get-tuple-element.67) | copy-start | bytes 4612
  20.0 15.4 %copy-start.20 = (f32[384]{0:T(512)}, f32[384]{0:T(512)S(1)}, u32[]{:S(2)}) copy-start(f32[384]{0:T(512)S(1)} %get-tuple-element.68) | copy-start | bytes 4612
  20.0 15.4 %copy-start.22 = (f32[384]{0:T(512)}, f32[384]{0:T(512)S(1)}, u32[]{:S(2)}) copy-start(f32[384]{0:T(512)S(1)} %get-tuple-element.69) | copy-start | bytes 4612
  20.0 15.4 %copy-start.24 = (f32[384]{0:T(512)}, f32[384]{0:T(512)S(1)}, u32[]{:S(2)}) copy-start(f32[384]{0:T(512)S(1)} %get-tuple-element.70) | copy-start | bytes 4612
  20.0 15.4 %copy-start.26 = (f32[384]{0:T(512)}, f32[384]{0:T(512)S(1)}, u32[]{:S(2)}) copy-start(f32[384]{0:T(512)S(1)} %get-tuple-element.71) | copy-start | bytes 4612
  20.0 15.4 %copy-start.28 = (f32[384]{0:T(512)}, f32[384]{0:T(512)S(1)}, u32[]{:S(2)}) copy-start(f32[384]{0:T(512)S(1)} %get-tuple-element.72) | copy-start | bytes 4612
  20.0 15.4 %copy-start.30 = (f32[384]{0:T(512)}, f32[384]{0:T(512)S(1)}, u32[]{:S(2)}) copy-start(f32[384]{0:T(512)S(1)} %get-tuple-element.73) | copy-start | bytes 4612
  20.0 15.4 %copy-start.32 = (f32[384]{0:T(512)}, f32[384]{0:T(512)S(1)}, u32[]{:S(2)}) copy-start(f32[384]{0:T(512)S(1)} %get-tuple-element.74) | copy-start | bytes 4612
  20.1 15.4 %copy-start.34 = (f32[384]{0:T(512)}, f32[384]{0:T(512)S(1)}, u32[]{:S(2)}) copy-start(f32[384]{0:T(512)S(1)} %get-tuple-element.75) | copy-start | bytes 4612
  20.1 15.4 %copy-start.36 = (f32[384]{0:T(512)}, f32[384]{0:T(512)S(1)}, u32[]{:S(2)}) copy-start(f32[384]{0:T(512)S(1)} %get-tuple-element.76) | copy-start | bytes 4612
  20.1 15.4 %copy-start.38 = (f32[384]{0:T(512)}, f32[384]{0:T(512)S(1)}, u32[]{:S(2)}) copy-start(f32[384]{0:T(512)S(1)} %get-tuple-element.77) | copy-start | bytes 4612
  20.1 15.4 %copy-start.40 = (f32[384]{0:T(512)}, f32[384]{0:T(512)S(1)}, u32[]{:S(2)}) copy-start(f32[384]{0:T(512)S(1)} %get-tuple-element.78) | copy-start | bytes 4612
  20.1 15.4 %copy-start.42 = (f32[384]{0:T(512)}, f32[384]{0:T(512)S(1)}, u32[]{:S(2)}) copy-start(f32[384]{0:T(512)S(1)} %get-tuple-element.79) | copy-start | bytes 4612
  20.1 15.4 %copy-start.44 = (f32[384]{0:T(512)}, f32[384]{0:T(512)S(1)}, u32[]{:S(2)}) copy-start(f32[384]{0:T(512)S(1)} %get-tuple-element.80) | copy-start | bytes 4612
  22.8 3.4 %copy-start.78 = (s32[1024]{0:T(1024)}, s32[1024]{0:T(1024)S(1)}, u32[]{:S(2)}) copy-start(s32[1024]{0:T(1024)S(1)} %pad_clamp_fusion.3) | copy-start | bytes 12292
  22.8 3.4 %copy-start.77 = (s32[1024]{0:T(1024)}, s32[1024]{0:T(1024)S(1)}, u32[]{:S(2)}) copy-start(s32[1024]{0:T(1024)S(1)} %pad_clamp_fusion.4) | copy-start | bytes 12292
  22.9 10.5 %copy-start.73 = (s32[1024]{0:T(1024)}, s32[1024]{0:T(1024)S(1)}, u32[]{:S(2)}) copy-start(s32[1024]{0:T(1024)S(1)} %pad_clamp_fusion.5) | copy-start | bytes 12292
  22.9 10.5 %copy-start.74 = (s32[1024]{0:T(1024)}, s32[1024]{0:T(1024)S(1)}, u32[]{:S(2)}) copy-start(s32[1024]{0:T(1024)S(1)} %pad_clamp_fusion.6) | copy-start | bytes 12292
  22.9 10.5 %copy-start.75 = (s32[1024]{0:T(1024)}, s32[1024]{0:T(1024)S(1)}, u32[]{:S(2)}) copy-start(s32[1024]{0:T(1024)S(1)} %pad_clamp_fusion.7) | copy-start | bytes 12292
  22.9 10.5 %copy-start.71 = (s32[1024]{0:T(1024)}, s32[1024]{0:T(1024)S(1)}, u32[]{:S(2)}) copy-start(s32[1024]{0:T(1024)S(1)} %pad_clamp_fusion) | copy-start | bytes 12292
  23.0 10.6 %copy-start.72 = (s32[1024]{0:T(1024)}, s32[1024]{0:T(1024)S(1)}, u32[]{:S(2)}) copy-start(s32[1024]{0:T(1024)S(1)} %pad_clamp_fusion.1) | copy-start | bytes 12292
  26.9 8.0 %copy-start.1 = (bf16[1,4,8,8,384]{4,3,2,1,0:T(8,128)(2,1)S(1)}, bf16[1,4,8,8,384]{4,3,2,1,0:T(8,128)(2,1)}, u32[]{:S(2)}) copy-start(bf16[1,4,8,8,384]{4,3,2,1,0:T(8,128)(2,1)} %param.19) | copy-start | bytes 589828
  29.3 6.0 %copy-start.76 = (s32[1024]{0:T(1024)}, s32[1024]{0:T(1024)S(1)}, u32[]{:S(2)}) copy-start(s32[1024]{0:T(1024)S(1)} %pad_clamp_fusion.2) | copy-start | bytes 12292
  32.8 2.7 %copy-start.46 = (f32[384]{0:T(512)S(1)}, f32[384]{0:T(512)}, u32[]{:S(2)}) copy-start(f32[384]{0:T(512)} %get-tuple-element.81) | copy-start | bytes 4612
  32.8 2.7 %copy-start.48 = (f32[384]{0:T(512)S(1)}, f32[384]{0:T(512)}, u32[]{:S(2)}) copy-start(f32[384]{0:T(512)} %get-tuple-element.82) | copy-start | bytes 4612
  32.8 2.7 %copy-start.50 = (f32[384]{0:T(512)S(1)}, f32[384]{0:T(512)}, u32[]{:S(2)}) copy-start(f32[384]{0:T(512)} %get-tuple-element.83) | copy-start | bytes 4612
  35.5 4.5 %copy-start.7 = (f32[384]{0:T(512)S(1)}, f32[384]{0:T(512)}, u32[]{:S(2)}) copy-start(f32[384]{0:T(512)} %param.26) | copy-start | bytes 4612
  45.3 3.1 %copy-start.2 = (f32[256,384]{1,0:T(8,128)}, f32[256,384]{1,0:T(8,128)S(1)}, u32[]{:S(2)}) copy-start(f32[256,384]{1,0:T(8,128)S(1)} %get-tuple-element.151) | copy-start | bytes 1179652
  48.5 134.3 %reduce-scatter.2.cloned.1.call-start = ((), (), s32[]{:S(2)}) async-start(), calls=%async_computation.2 | async-start | bytes 2506752 | tf_op jit(solution)/shard_map/reduce_scatter | solution.py:162
  56.1 114.7 %collective-permute-start.2 = (bf16[4,3,8,384]{3,2,1,0:T(8,128)(2,1)}, bf16[4,3,8,384]{3,2,1,0:T(8,128)(2,1)S(1)}, u32[]{:S(2)}, u32[]{:S(2)}) collective-permute-start(bf16[4,3,8,384]{3,2,1,0:T(8,128)(2,1)} %get-tuple-element.144), channel_id=1, source_target_pairs={{0,1},{1,2},{2,3},{3,4},{4,5},{5,6},{6,7},{7,8},{8,9},{9,10},{10,1... | collective-permute-start | bytes 221192 | tf_op jit(solution)/shard_map/ppermute | solution.py:13
  61.2 111.7 %collective-permute-start.3 = (bf16[4,3,8,384]{3,2,1,0:T(8,128)(2,1)S(1)}, bf16[4,3,8,384]{3,2,1,0:T(8,128)(2,1)S(1)}, u32[]{:S(2)}, u32[]{:S(2)}) collective-permute-start(bf16[4,3,8,384]{3,2,1,0:T(8,128)(2,1)S(1)} %get-tuple-element.145), channel_id=1, source_target_pairs={{1,0},{2,1},{3,2},{4,3},{5,4},{6,5},{7,6},{8,7},{9,8},{10,9},{11,1... | collective-permute-start | bytes 221192 | tf_op jit(solution)/shard_map/ppermute | solution.py:13
  102.3 72.7 %copy-start.90 = (pred[4]{0:T(512)(128)(4,1)S(1)}, pred[4]{0:T(512)(128)(4,1)}, u32[]{:S(2)}) copy-start(pred[4]{0:T(512)(128)(4,1)} %copy-done.89) | copy-start | bytes 16
  170.8 5.0 %copy-start.88 = (pred[4]{0:T(512)(128)(4,1)S(1)}, pred[4]{0:T(512)(128)(4,1)}, u32[]{:S(2)}) copy-start(pred[4]{0:T(512)(128)(4,1)} %copy-done.87) | copy-start | bytes 16
  170.8 5.0 %copy-start.100 = (pred[4]{0:T(512)(128)(4,1)S(1)}, pred[4]{0:T(512)(128)(4,1)}, u32[]{:S(2)}) copy-start(pred[4]{0:T(512)(128)(4,1)} %copy-done.99) | copy-start | bytes 16
  170.8 5.1 %copy-start.86 = (pred[4]{0:T(512)(128)(4,1)S(1)}, pred[4]{0:T(512)(128)(4,1)}, u32[]{:S(2)}) copy-start(pred[4]{0:T(512)(128)(4,1)} %copy-done.85) | copy-start | bytes 16
  170.8 5.1 %copy-start.98 = (pred[4]{0:T(512)(128)(4,1)S(1)}, pred[4]{0:T(512)(128)(4,1)}, u32[]{:S(2)}) copy-start(pred[4]{0:T(512)(128)(4,1)} %copy-done.97) | copy-start | bytes 16
  170.8 5.2 %copy-start.84 = (pred[4]{0:T(512)(128)(4,1)S(1)}, pred[4]{0:T(512)(128)(4,1)}, u32[]{:S(2)}) copy-start(pred[4]{0:T(512)(128)(4,1)} %copy-done.83) | copy-start | bytes 16
  171.5 5.3 %copy-start.82 = (pred[4]{0:T(512)(128)(4,1)S(1)}, pred[4]{0:T(512)(128)(4,1)}, u32[]{:S(2)}) copy-start(pred[4]{0:T(512)(128)(4,1)} %copy-done.81) | copy-start | bytes 16
  171.6 5.3 %copy-start.96 = (pred[4]{0:T(512)(128)(4,1)S(1)}, pred[4]{0:T(512)(128)(4,1)}, u32[]{:S(2)}) copy-start(pred[4]{0:T(512)(128)(4,1)} %copy-done.95) | copy-start | bytes 16
  172.3 4.7 %copy-start.80 = (pred[4]{0:T(512)(128)(4,1)S(1)}, pred[4]{0:T(512)(128)(4,1)}, u32[]{:S(2)}) copy-start(pred[4]{0:T(512)(128)(4,1)} %copy-done.79) | copy-start | bytes 16
  172.3 4.7 %copy-start.94 = (pred[4]{0:T(512)(128)(4,1)S(1)}, pred[4]{0:T(512)(128)(4,1)}, u32[]{:S(2)}) copy-start(pred[4]{0:T(512)(128)(4,1)} %copy-done.93) | copy-start | bytes 16
  (54 other events, 59.8 us)
Sparse Core Ops, SparseCore 0:
  48.6 47.5 all-reduce.3
  100.6 63.7 reduce-scatter.1
where the time goes:
time: 191 us; the launch traced here: 190 us
  blocking collectives  68.5 us (36%)
  other arithmetic  31.7 us (17%)
  waiting for transfers between devices  31.3 us (16%)
  local copies, waits for them, and re-layouts  19.6 us (10%)
  between operations  17.1 us (9%)
  matrix products  11 us (6%)
  starting transfers between devices  10.4 us (5%)
    psum x1, blocking collectives, per_device(): embedding = lax.psum(emb_term, 'space')  61 us
    psum x1, waiting for transfers between devices, per_device(): lax.psum(local_weight.astype(jnp.bfloat16), 'dp').astype(jnp.float32)  31.3 us
    gather x16, local copies, waits for them, and re-layouts, pick(): chosen = jnp.take(source, index, axis=0)  10.5 us
    ppermute x4, starting transfers between devices, passed_along(): lax.ppermute(value, axis, [(source, source + steps) for source in range(l...  10.3 us
    psum x1, blocking collectives, per_device(): lax.psum(kernel_grad.astype(jnp.bfloat16), 'dp').astype(jnp.float32)  7.44 us
    select_n x16, other arithmetic, pick(): return jnp.where(valid[:, None, None, None], chosen, jnp.zeros_like(chosen))  6.9 us
    slice x3, local copies, waits for them, and re-layouts, depthwise(): total = total + window * kernel[row_tap, col_tap]  4.74 us
    broadcast_in_dim x1, other arithmetic, per_device(): return (embedding[None, :], grad_tiles[None], weight_share, kernel_total)  4.44 us
  transfers between devices with their start and end apart: 6, of which 1 were waited for; matrix products, arithmetic and copies ran while one was open for 24% of the time, Pallas kernels for 0%

commit v1 on v0

--- a/solution.py
+++ b/solution.py
@@ -151,7 +151,11 @@
         w_out,
         layer_scale,
     )
-    embedding = lax.psum(emb_term, "space")
+    embedding = emb_term
+    for hop in (1, 2, 4, 8):
+        embedding = embedding + lax.ppermute(
+            embedding, "space", [(dev, dev ^ hop) for dev in range(16)]
+        )
     local_weight = lax.dot_general(
         activated, grad_mixed, (((0,), (0,)), ((), ())), preferred_element_type=jnp.float32
     )

time: 191 us -> 222 us (1.16)
  waiting for transfers between devices: 31.3 us -> 41.8 us
  other arithmetic: 31.7 us -> 41.8 us
  starting transfers between devices: 10.4 us -> 16.3 us
  local copies, waits for them, and re-layouts: 19.6 us -> 24.5 us
    psum x1, waiting for transfers between devices: 31.3 us -> 40.7 us  [per_device(): lax.psum(local_weight.astype(jnp.bfloat16), 'dp').astype(jnp.float32)]
    ppermute x0 -> x4, starting transfers between devices: none -> 7.44 us  [per_device(): lax.ppermute(embedding, 'space', [(dev, dev ^ hop) for dev in range(16)])]
    select_n x16, other arithmetic: 6.9 us -> 12 us  [pick(): return jnp.where(valid[:, None, None, None], chosen, jnp.zeros_like(chosen))]
    gather x8, other arithmetic: 0.05 us -> 4.17 us
  transfers between devices with their start and end apart: 6 -> 10, of which waited for: 1 -> 2; matrix products, arithmetic and copies ran while one was open for 24% -> 23% of each run, Pallas kernels for 0% -> 0%
where the time goes in v1:
time: 222 us; the launch traced here: 220 us
  blocking collectives  66.9 us (30%)
  other arithmetic  41.8 us (19%)
  waiting for transfers between devices  41.8 us (19%)
  local copies, waits for them, and re-layouts  24.5 us (11%)
  between operations  17.3 us (8%)
  starting transfers between devices  16.3 us (7%)
  matrix products  11.7 us (5%)
    psum x1, blocking collectives, per_device(): kernel_total = lax.psum(kernel_dp, 'space')  59.3 us
    psum x1, waiting for transfers between devices, per_device(): lax.psum(local_weight.astype(jnp.bfloat16), 'dp').astype(jnp.float32)  40.7 us
    select_n x16, other arithmetic, pick(): return jnp.where(valid[:, None, None, None], chosen, jnp.zeros_like(chosen))  12 us
    gather x16, local copies, waits for them, and re-layouts, pick(): chosen = jnp.take(source, index, axis=0)  11.2 us
    ppermute x4, starting transfers between devices, passed_along(): lax.ppermute(value, axis, [(source, source + steps) for source in range(l...  8.82 us
    psum x1, blocking collectives, per_device(): lax.psum(kernel_grad.astype(jnp.bfloat16), 'dp').astype(jnp.float32)  7.64 us
    ppermute x4, starting transfers between devices, per_device(): lax.ppermute(embedding, 'space', [(dev, dev ^ hop) for dev in range(16)])  7.44 us
    slice x3, local copies, waits for them, and re-layouts, depthwise(): total = total + window * kernel[row_tap, col_tap]  4.69 us
  transfers between devices with their start and end apart: 10, of which 2 were waited for; matrix products, arithmetic and copies ran while one was open for 23% of the time, Pallas kernels for 0%

profile of v1, /device:TPU:0, one launch (start us, length us, event | category | flops | bytes accessed | tf_op | source)
XLA Modules:
  0.0 220.4 jit_solution(10294338647452512274)
XLA Ops:
  7.3 1.1 fusion.191
  8.3 1.3 collective-permute-start.1
  9.6 3.0 %collective-permute-start = (bf16[4,3,8,384]{3,2,1,0:T(8,128)(2,1)S(1)}, bf16[4,3,8,384]{3,2,1,0:T(8,128)(2,1)S(1)}, u32[]{:S(2)}, u32[]{:S(2)}) collective-permute-start(bf16[4,3,8,384]{3,2,1,0:T(8,128)(2,1)S(1)} %get-tuple-element.144), channel_id=1, source_target_pairs={{0,1},{1,2},{2,3},{3,4},{4,5},{5,6},{6,7},{7,8},{8,9},{9,10},{10,1... | collective-permute-start | bytes 221192 | tf_op jit(solution)/shard_map/ppermute | solution.py:13
  12.7 1.1 fusion.192
  13.8 1.8 compare_reduce_fusion.7
  15.6 1.3 clamp_reduce_fusion.7
  19.3 1.3 slice_reduce_fusion.47
  20.7 1.8 slice_reduce_fusion.48
  22.7 1.6 slice_reduce_fusion.46
  29.1 0.7 mul.1256
  30.5 0.8 gather_fusion.4
  31.9 0.8 select_select_fusion.5
  32.7 0.8 select_select_fusion.4
  33.5 0.8 fusion.169
  34.9 0.7 gather_fusion.6
  35.6 0.8 select_select_fusion.6
  36.4 0.7 gather_fusion.1
  37.1 0.8 select_select_fusion.7
  37.9 0.7 gather_fusion.7
  38.5 0.7 fusion.180
  39.3 0.7 gather_fusion.2
  40.0 0.8 fusion.182
  40.7 0.7 gather_fusion.5
  41.4 0.7 fusion.181
  42.1 0.7 gather_fusion
  42.8 0.7 fusion.183
  44.4 4.1 %fusion.187 = (f32[4,8,8]{2,1,0:T(8,128)S(1)}, f32[4,8,8,384]{3,2,1,0:T(8,128)S(1)}) fusion(f32[384]{0:T(512)} %get-tuple-element.114, bf16[4,11,14,384]{3,2,1,0:T(8,128)(2,1)S(1)} %get-tuple-element.141, f32[384]{0:T(512)} %get-tuple-element.115, f32[384]{0:T(512)S(1)} %get-tuple-element.68, f32[384]{0:T(512)S(1)} %get-tuple-element.69, ...), kind=kLoop, calls=%fused_computation.495 | loop fusion | flops 16219904 | bytes 9071104 | tf_op jit(solution)/shard_map/reduce_sum | solution.py:67
  48.9 2.0 multiply_convert_fusion
  50.9 3.1 %multiply_reduce_fusion.1 = (f32[256]{0:T(256)S(1)}, f32[256,384]{1,0:T(8,128)S(1)}) fusion(f32[384]{0:T(512)S(1)} %copy-done.12, bf16[384,1536]{1,0:T(8,128)(2,1)S(1)} %copy-done, bf16[256,384]{1,0:T(8,128)(2,1)S(1)} %copy-done.6, bf16[1536,384]{1,0:T(8,128)(2,1)} %param.28, f32[256,1536]{1,0:T(8,128)} %get-tuple-element.151), kind=kOutput, calls=%fused_computation.359 | convolution fusion | flops 608108288 | bytes 4524544 | tf_op jit(solution)/shard_map/dot_general | solution.py:86
  54.8 0.7 div.33
  55.5 2.7 %convolution_convert_fusion = bf16[1536,384]{1,0:T(8,128)(2,1)} fusion(bf16[256,1536]{1,0:T(8,128)(2,1)} %get-tuple-element.150, bf16[256,384]{1,0:T(8,128)(2,1)S(1)} %copy-done.6), kind=kOutput, calls=%fused_computation.16 | convolution fusion | flops 302579712 | bytes 2162688 | tf_op jit(solution)/shard_map/dot_general | solution.py:159
  58.3 2.6 %fusion.103 = (bf16[384]{0:T(512)(128)(2,1)}, bf16[384]{0:T(512)(128)(2,1)}, bf16[384]{0:T(512)(128)(2,1)}, bf16[384]{0:T(512)(128)(2,1)}, bf16[384]{0:T(512)(12...) fusion(bf16[4,11,14,384]{3,2,1,0:T(8,128)(2,1)S(1)} %get-tuple-, ...), kind=kLoop, calls=%fused_computation.243 | loop fusion | flops 5989632 | bytes 4738048 | tf_op jit(solution)/shard_map/reduce_sum | solution.py:101
  60.9 1.6 fusion.53
  63.2 0.8 fusion.189
  64.0 40.7 %all-reduce.3.cloned.1.call-done = bf16[1536,384]{1,0:T(8,128)(2,1)} async-done(((bf16[1536,384]{1,0:T(8,128)(2,1)}), bf16[1536,384]{1,0:T(8,128)(2,1)}) %all-reduce.3.cloned.1.call-update) | async-done | bytes 1179664 | tf_op jit(solution)/shard_map/psum | solution.py:163
  104.7 2.8 %convert_element_type.315 = f32[1536,384]{1,0:T(8,128)} convert(bf16[1536,384]{1,0:T(8,128)(2,1)} %all-reduce.3.cloned.1.call-done) | non-fusion elementwise | flops 589824 | bytes 3538944 | tf_op jit(solution)/shard_map/convert_element_type | solution.py:163
  107.8 0.9 copy-done.1
  108.8 3.9 %fusion.85 = (bf16[384]{0:T(512)(128)(2,1)}, bf16[384]{0:T(512)(128)(2,1)}, bf16[384]{0:T(512)(128)(2,1)}, bf16[384]{0:T(512)(128)(2,1)}, bf16[384]{0:T(512)(128...) fusion(f32[4,8,8,384]{3,2,1,0:T(8,128)S(1)} %get-tuple-element., ...), kind=kOutput, calls=%fused_computation.225 | convolution fusion | flops 306998016 | bytes 3505152 | tf_op jit(solution)/shard_map/dot_general | solution.py:74
  114.0 1.3 collective-permute-start.7
  115.3 3.2 %collective-permute-start.6 = (bf16[4,3,8,384]{3,2,1,0:T(8,128)(2,1)}, bf16[4,3,8,384]{3,2,1,0:T(8,128)(2,1)S(1)}, u32[]{:S(2)}, u32[]{:S(2)}) collective-permute-start(bf16[4,3,8,384]{3,2,1,0:T(8,128)(2,1)} %get-tuple-element.142), channel_id=1, source_target_pairs={{0,1},{1,2},{2,3},{3,4},{4,5},{5,6},{6,7},{7,8},{8,9},{9,10},{10,1... | collective-permute-start | bytes 221192 | tf_op jit(solution)/shard_map/ppermute | solution.py:13
  118.6 0.8 gather_fusion.12
  119.4 0.8 gather_fusion.11
  120.2 0.7 multiply_reduce_fusion.3
  120.9 1.1 collective-permute-start.2
  122.0 0.8 select_select_fusion
  122.8 0.8 select_select_fusion.1
  123.9 2.3 %collective-permute-start.3 = (f32[384]{0:T(512)S(1)}, f32[384]{0:T(512)S(1)}, u32[]{:S(2)}, u32[]{:S(2)}) collective-permute-start(f32[384]{0:T(512)S(1)} %fusion.186), channel_id=1, source_target_pairs={{0,2},{1,3},{2,0},{3,1},{4,6},{5,7},{6,4},{7,5},{8,10},{9,11},{10,... | collective-permute-start | bytes 4616 | tf_op jit(solution)/shard_map/ppermute | solution.py:156
  126.8 1.0 collective-permute-done.3
  127.8 1.5 collective-permute-start.4
  129.3 7.6 %psum.22 = bf16[7,7,384]{2,1,0:T(8,128)(2,1)S(1)} all-reduce(bf16[7,7,384]{2,1,0:T(8,128)(2,1)S(1)} %convert_element_type.316), channel_id=1, replica_groups=mesh['dp'=2,'space'=16] {'dp'}, use_global_device_ids=true, to_apply=%region_57.62 | all-reduce | flops 18816 | bytes 75264 | tf_op jit(solution)/shard_map/psum | solution.py:164
  136.9 2.5 %collective-permute-start.5 = (f32[384]{0:T(512)S(1)}, f32[384]{0:T(512)S(1)}, u32[]{:S(2)}, u32[]{:S(2)}) collective-permute-start(f32[384]{0:T(512)S(1)} %add.419), channel_id=1, source_target_pairs={{0,8},{1,9},{2,10},{3,11},{4,12},{5,13},{6,14},{7,15},{8,0},{9,1},... | collective-permute-start | bytes 4616 | tf_op jit(solution)/shard_map/ppermute | solution.py:156
  139.5 59.3 %all-reduce.4 = f32[7,7,384]{2,1,0:T(8,128)} all-reduce(bf16[7,7,384]{2,1,0:T(8,128)(2,1)S(1)} %psum.22), channel_id=1, replica_groups=mesh['dp'=2,'space'=16] {'space'}, use_global_device_ids=true, to_apply=%region_58.63 | all-reduce | flops 18816 | bytes 112896 | tf_op jit(solution)/shard_map/psum | solution.py:167
  199.4 0.7 gather_fusion.14
  200.1 0.7 gather_fusion.15
  200.7 0.7 gather_fusion.13
  201.5 0.7 gather_fusion.9
  202.1 0.7 gather_fusion.8
  203.5 0.7 fusion.176
  204.2 0.7 fusion.177
  205.0 0.7 fusion.179
  205.7 0.8 fusion.178
  206.4 0.8 select_select_fusion.2
  207.2 0.8 select_select_fusion.3
  209.2 4.4 %fusion.175 = bf16[1,4,8,8,384]{4,3,2,1,0:T(8,128)(2,1)} fusion(f32[384]{0:T(512)S(1)} %copy-done.52, f32[4,11,14,384]{3,2,1,0:T(8,128)S(1)} %get-tuple-element.136, f32[384]{0:T(512)S(1)} %copy-done.14, f32[384]{0:T(512)} %get-tuple-element.105, f32[384]{0:T(512)} %get-tuple-element.113, f32[384]{0:T(512)} %get-tuple-element.112, ...), kind=kLoop, calls=%fused_computation.371 | loop fusion | flops 10715136 | bytes 17677840 | tf_op jit(solution)/shard_map/broadcast_in_dim | solution.py:187
  (373 shorter events, 14.6 us)
Async XLA Ops:
  7.2 41.7 %copy-start = (bf16[384,1536]{1,0:T(8,128)(2,1)S(1)}, bf16[384,1536]{1,0:T(8,128)(2,1)}, u32[]{:S(2)}) copy-start(bf16[384,1536]{1,0:T(8,128)(2,1)} %param.27) | copy-start | bytes 3538948
  7.2 24.1 %copy-start.132 = (f32[1,384]{1,0:T(1,128)S(1)}, f32[1,384]{1,0:T(1,128)}, u32[]{:S(2)}) copy-start(f32[1,384]{1,0:T(1,128)} %param.22) | copy-start | bytes 4612
  7.2 24.1 %copy-start.133 = (f32[1,4]{1,0:T(1,128)S(1)}, f32[1,4]{1,0:T(1,128)}, u32[]{:S(2)}) copy-start(f32[1,4]{1,0:T(1,128)} %param.21) | copy-start | bytes 52
  7.2 26.3 %copy-start.4 = (bf16[1,4,8,8,384]{4,3,2,1,0:T(8,128)(2,1)S(1)}, bf16[1,4,8,8,384]{4,3,2,1,0:T(8,128)(2,1)}, u32[]{:S(2)}) copy-start(bf16[1,4,8,8,384]{4,3,2,1,0:T(8,128)(2,1)} %param.20) | copy-start | bytes 589828
  7.2 26.3 %copy-start.87 = (f32[384]{0:T(512)S(1)}, f32[384]{0:T(512)}, u32[]{:S(2)}) copy-start(f32[384]{0:T(512)} %param.29) | copy-start | bytes 4612
  7.2 97.5 %all-reduce.3.cloned.1.call-start = ((), (), s32[]{:S(2)}) async-start(), calls=%async_computation.1 | async-start | bytes 2359296 | tf_op jit(solution)/shard_map/psum | solution.py:163
  8.3 26.6 %collective-permute-start.1 = (bf16[4,3,8,384]{3,2,1,0:T(8,128)(2,1)S(1)}, bf16[4,3,8,384]{3,2,1,0:T(8,128)(2,1)S(1)}, u32[]{:S(2)}, u32[]{:S(2)}) collective-permute-start(bf16[4,3,8,384]{3,2,1,0:T(8,128)(2,1)S(1)} %get-tuple-element.145), channel_id=1, source_target_pairs={{1,0},{2,1},{3,2},{4,3},{5,4},{6,5},{7,6},{8,7},{9,8},{10,9},{11,1... | collective-permute-start | bytes 221192 | tf_op jit(solution)/shard_map/ppermute | solution.py:13
  9.6 26.8 %collective-permute-start = (bf16[4,3,8,384]{3,2,1,0:T(8,128)(2,1)S(1)}, bf16[4,3,8,384]{3,2,1,0:T(8,128)(2,1)S(1)}, u32[]{:S(2)}, u32[]{:S(2)}) collective-permute-start(bf16[4,3,8,384]{3,2,1,0:T(8,128)(2,1)S(1)} %get-tuple-element.144), channel_id=1, source_target_pairs={{0,1},{1,2},{2,3},{3,4},{4,5},{5,6},{6,7},{7,8},{8,9},{9,10},{10,1... | collective-permute-start | bytes 221192 | tf_op jit(solution)/shard_map/ppermute | solution.py:13
  20.5 23.5 %copy-start.13 = (f32[384]{0:T(512)}, f32[384]{0:T(512)S(1)}, u32[]{:S(2)}) copy-start(f32[384]{0:T(512)S(1)} %get-tuple-element.86) | copy-start | bytes 4612
  20.6 23.5 %copy-start.15 = (f32[384]{0:T(512)}, f32[384]{0:T(512)S(1)}, u32[]{:S(2)}) copy-start(f32[384]{0:T(512)S(1)} %get-tuple-element.87) | copy-start | bytes 4612
  20.6 23.5 %copy-start.17 = (f32[384]{0:T(512)}, f32[384]{0:T(512)S(1)}, u32[]{:S(2)}) copy-start(f32[384]{0:T(512)S(1)} %get-tuple-element.88) | copy-start | bytes 4612
  20.6 23.5 %copy-start.19 = (f32[384]{0:T(512)}, f32[384]{0:T(512)S(1)}, u32[]{:S(2)}) copy-start(f32[384]{0:T(512)S(1)} %get-tuple-element.89) | copy-start | bytes 4612
  20.6 23.5 %copy-start.21 = (f32[384]{0:T(512)}, f32[384]{0:T(512)S(1)}, u32[]{:S(2)}) copy-start(f32[384]{0:T(512)S(1)} %get-tuple-element.90) | copy-start | bytes 4612
  20.6 23.5 %copy-start.23 = (f32[384]{0:T(512)}, f32[384]{0:T(512)S(1)}, u32[]{:S(2)}) copy-start(f32[384]{0:T(512)S(1)} %get-tuple-element.91) | copy-start | bytes 4612
  20.6 23.5 %copy-start.25 = (f32[384]{0:T(512)}, f32[384]{0:T(512)S(1)}, u32[]{:S(2)}) copy-start(f32[384]{0:T(512)S(1)} %get-tuple-element.92) | copy-start | bytes 4612
  20.6 23.5 %copy-start.27 = (f32[384]{0:T(512)}, f32[384]{0:T(512)S(1)}, u32[]{:S(2)}) copy-start(f32[384]{0:T(512)S(1)} %get-tuple-element.93) | copy-start | bytes 4612
  20.6 23.5 %copy-start.29 = (f32[384]{0:T(512)}, f32[384]{0:T(512)S(1)}, u32[]{:S(2)}) copy-start(f32[384]{0:T(512)S(1)} %get-tuple-element.94) | copy-start | bytes 4612
  20.6 23.5 %copy-start.31 = (f32[384]{0:T(512)}, f32[384]{0:T(512)S(1)}, u32[]{:S(2)}) copy-start(f32[384]{0:T(512)S(1)} %get-tuple-element.95) | copy-start | bytes 4612
  20.6 23.5 %copy-start.33 = (f32[384]{0:T(512)}, f32[384]{0:T(512)S(1)}, u32[]{:S(2)}) copy-start(f32[384]{0:T(512)S(1)} %get-tuple-element.96) | copy-start | bytes 4612
  20.7 23.5 %copy-start.35 = (f32[384]{0:T(512)}, f32[384]{0:T(512)S(1)}, u32[]{:S(2)}) copy-start(f32[384]{0:T(512)S(1)} %get-tuple-element.97) | copy-start | bytes 4612
  20.7 23.5 %copy-start.37 = (f32[384]{0:T(512)}, f32[384]{0:T(512)S(1)}, u32[]{:S(2)}) copy-start(f32[384]{0:T(512)S(1)} %get-tuple-element.98) | copy-start | bytes 4612
  20.7 23.5 %copy-start.39 = (f32[384]{0:T(512)}, f32[384]{0:T(512)S(1)}, u32[]{:S(2)}) copy-start(f32[384]{0:T(512)S(1)} %get-tuple-element.99) | copy-start | bytes 4612
  20.7 23.5 %copy-start.41 = (f32[384]{0:T(512)}, f32[384]{0:T(512)S(1)}, u32[]{:S(2)}) copy-start(f32[384]{0:T(512)S(1)} %get-tuple-element.100) | copy-start | bytes 4612
  20.7 23.5 %copy-start.43 = (f32[384]{0:T(512)}, f32[384]{0:T(512)S(1)}, u32[]{:S(2)}) copy-start(f32[384]{0:T(512)S(1)} %get-tuple-element.101) | copy-start | bytes 4612
  20.7 23.5 %copy-start.45 = (f32[384]{0:T(512)}, f32[384]{0:T(512)S(1)}, u32[]{:S(2)}) copy-start(f32[384]{0:T(512)S(1)} %get-tuple-element.102) | copy-start | bytes 4612
  20.7 23.5 %copy-start.47 = (f32[384]{0:T(512)}, f32[384]{0:T(512)S(1)}, u32[]{:S(2)}) copy-start(f32[384]{0:T(512)S(1)} %get-tuple-element.103) | copy-start | bytes 4612
  20.7 23.5 %copy-start.49 = (f32[384]{0:T(512)}, f32[384]{0:T(512)S(1)}, u32[]{:S(2)}) copy-start(f32[384]{0:T(512)S(1)} %get-tuple-element.104) | copy-start | bytes 4612
  22.5 21.6 %copy-start.51 = (f32[384]{0:T(512)}, f32[384]{0:T(512)S(1)}, u32[]{:S(2)}) copy-start(f32[384]{0:T(512)S(1)} %get-tuple-element.67) | copy-start | bytes 4612
  22.5 21.7 %copy-start.53 = (f32[384]{0:T(512)}, f32[384]{0:T(512)S(1)}, u32[]{:S(2)}) copy-start(f32[384]{0:T(512)S(1)} %get-tuple-element.68) | copy-start | bytes 4612
  22.5 21.7 %copy-start.55 = (f32[384]{0:T(512)}, f32[384]{0:T(512)S(1)}, u32[]{:S(2)}) copy-start(f32[384]{0:T(512)S(1)} %get-tuple-element.69) | copy-start | bytes 4612
  22.5 21.7 %copy-start.57 = (f32[384]{0:T(512)}, f32[384]{0:T(512)S(1)}, u32[]{:S(2)}) copy-start(f32[384]{0:T(512)S(1)} %get-tuple-element.70) | copy-start | bytes 4612
  22.6 21.7 %copy-start.59 = (f32[384]{0:T(512)}, f32[384]{0:T(512)S(1)}, u32[]{:S(2)}) copy-start(f32[384]{0:T(512)S(1)} %get-tuple-element.71) | copy-start | bytes 4612
  22.6 21.7 %copy-start.61 = (f32[384]{0:T(512)}, f32[384]{0:T(512)S(1)}, u32[]{:S(2)}) copy-start(f32[384]{0:T(512)S(1)} %get-tuple-element.72) | copy-start | bytes 4612
  22.6 21.7 %copy-start.63 = (f32[384]{0:T(512)}, f32[384]{0:T(512)S(1)}, u32[]{:S(2)}) copy-start(f32[384]{0:T(512)S(1)} %get-tuple-element.73) | copy-start | bytes 4612
  22.6 21.7 %copy-start.65 = (f32[384]{0:T(512)}, f32[384]{0:T(512)S(1)}, u32[]{:S(2)}) copy-start(f32[384]{0:T(512)S(1)} %get-tuple-element.74) | copy-start | bytes 4612
  22.6 21.7 %copy-start.67 = (f32[384]{0:T(512)}, f32[384]{0:T(512)S(1)}, u32[]{:S(2)}) copy-start(f32[384]{0:T(512)S(1)} %get-tuple-element.75) | copy-start | bytes 4612
  22.6 21.7 %copy-start.69 = (f32[384]{0:T(512)}, f32[384]{0:T(512)S(1)}, u32[]{:S(2)}) copy-start(f32[384]{0:T(512)S(1)} %get-tuple-element.76) | copy-start | bytes 4612
  22.6 21.7 %copy-start.71 = (f32[384]{0:T(512)}, f32[384]{0:T(512)S(1)}, u32[]{:S(2)}) copy-start(f32[384]{0:T(512)S(1)} %get-tuple-element.77) | copy-start | bytes 4612
  22.6 21.7 %copy-start.73 = (f32[384]{0:T(512)}, f32[384]{0:T(512)S(1)}, u32[]{:S(2)}) copy-start(f32[384]{0:T(512)S(1)} %get-tuple-element.78) | copy-start | bytes 4612
  22.6 21.7 %copy-start.75 = (f32[384]{0:T(512)}, f32[384]{0:T(512)S(1)}, u32[]{:S(2)}) copy-start(f32[384]{0:T(512)S(1)} %get-tuple-element.79) | copy-start | bytes 4612
  22.6 21.7 %copy-start.77 = (f32[384]{0:T(512)}, f32[384]{0:T(512)S(1)}, u32[]{:S(2)}) copy-start(f32[384]{0:T(512)S(1)} %get-tuple-element.80) | copy-start | bytes 4612
  22.6 21.7 %copy-start.79 = (f32[384]{0:T(512)}, f32[384]{0:T(512)S(1)}, u32[]{:S(2)}) copy-start(f32[384]{0:T(512)S(1)} %get-tuple-element.81) | copy-start | bytes 4612
  22.7 21.7 %copy-start.81 = (f32[384]{0:T(512)}, f32[384]{0:T(512)S(1)}, u32[]{:S(2)}) copy-start(f32[384]{0:T(512)S(1)} %get-tuple-element.82) | copy-start | bytes 4612
  22.7 21.7 %copy-start.83 = (f32[384]{0:T(512)}, f32[384]{0:T(512)S(1)}, u32[]{:S(2)}) copy-start(f32[384]{0:T(512)S(1)} %get-tuple-element.83) | copy-start | bytes 4612
  22.7 21.7 %copy-start.85 = (f32[384]{0:T(512)}, f32[384]{0:T(512)S(1)}, u32[]{:S(2)}) copy-start(f32[384]{0:T(512)S(1)} %get-tuple-element.84) | copy-start | bytes 4612
  58.3 155.3 %reduce-scatter.2.cloned.1.call-start = ((), (), s32[]{:S(2)}) async-start(), calls=%async_computation.2 | async-start | bytes 2506752 | tf_op jit(solution)/shard_map/reduce_scatter | solution.py:166
  112.9 13.4 %copy-start.125 = (bf16[384]{0:T(512)(128)(2,1)S(1)}, bf16[384]{0:T(512)(128)(2,1)}, u32[]{:S(2)}) copy-start(bf16[384]{0:T(512)(128)(2,1)} %get-tuple-element.18) | copy-start | bytes 2308
  112.9 13.4 %copy-start.124 = (bf16[384]{0:T(512)(128)(2,1)S(1)}, bf16[384]{0:T(512)(128)(2,1)}, u32[]{:S(2)}) copy-start(bf16[384]{0:T(512)(128)(2,1)} %get-tuple-element.17) | copy-start | bytes 2308
  112.9 13.4 %copy-start.123 = (bf16[384]{0:T(512)(128)(2,1)S(1)}, bf16[384]{0:T(512)(128)(2,1)}, u32[]{:S(2)}) copy-start(bf16[384]{0:T(512)(128)(2,1)} %get-tuple-element.16) | copy-start | bytes 2308
  112.9 13.5 %copy-start.122 = (bf16[384]{0:T(512)(128)(2,1)S(1)}, bf16[384]{0:T(512)(128)(2,1)}, u32[]{:S(2)}) copy-start(bf16[384]{0:T(512)(128)(2,1)} %get-tuple-element.15) | copy-start | bytes 2308
  112.9 13.5 %copy-start.121 = (bf16[384]{0:T(512)(128)(2,1)S(1)}, bf16[384]{0:T(512)(128)(2,1)}, u32[]{:S(2)}) copy-start(bf16[384]{0:T(512)(128)(2,1)} %get-tuple-element.14) | copy-start | bytes 2308
  112.9 13.5 %copy-start.120 = (bf16[384]{0:T(512)(128)(2,1)S(1)}, bf16[384]{0:T(512)(128)(2,1)}, u32[]{:S(2)}) copy-start(bf16[384]{0:T(512)(128)(2,1)} %get-tuple-element.13) | copy-start | bytes 2308
  112.9 13.5 %copy-start.119 = (bf16[384]{0:T(512)(128)(2,1)S(1)}, bf16[384]{0:T(512)(128)(2,1)}, u32[]{:S(2)}) copy-start(bf16[384]{0:T(512)(128)(2,1)} %get-tuple-element.12) | copy-start | bytes 2308
  112.9 13.5 %copy-start.118 = (bf16[384]{0:T(512)(128)(2,1)S(1)}, bf16[384]{0:T(512)(128)(2,1)}, u32[]{:S(2)}) copy-start(bf16[384]{0:T(512)(128)(2,1)} %get-tuple-element.11) | copy-start | bytes 2308
  112.9 13.5 %copy-start.117 = (bf16[384]{0:T(512)(128)(2,1)S(1)}, bf16[384]{0:T(512)(128)(2,1)}, u32[]{:S(2)}) copy-start(bf16[384]{0:T(512)(128)(2,1)} %get-tuple-element.10) | copy-start | bytes 2308
  112.9 13.5 %copy-start.116 = (bf16[384]{0:T(512)(128)(2,1)S(1)}, bf16[384]{0:T(512)(128)(2,1)}, u32[]{:S(2)}) copy-start(bf16[384]{0:T(512)(128)(2,1)} %get-tuple-element.9) | copy-start | bytes 2308
  113.0 13.5 %copy-start.115 = (bf16[384]{0:T(512)(128)(2,1)S(1)}, bf16[384]{0:T(512)(128)(2,1)}, u32[]{:S(2)}) copy-start(bf16[384]{0:T(512)(128)(2,1)} %get-tuple-element.8) | copy-start | bytes 2308
  113.0 13.3 %copy-start.126 = (bf16[384]{0:T(512)(128)(2,1)S(1)}, bf16[384]{0:T(512)(128)(2,1)}, u32[]{:S(2)}) copy-start(bf16[384]{0:T(512)(128)(2,1)} %get-tuple-element.19) | copy-start | bytes 2308
  114.0 85.3 %collective-permute-start.7 = (bf16[4,3,8,384]{3,2,1,0:T(8,128)(2,1)}, bf16[4,3,8,384]{3,2,1,0:T(8,128)(2,1)S(1)}, u32[]{:S(2)}, u32[]{:S(2)}) collective-permute-start(bf16[4,3,8,384]{3,2,1,0:T(8,128)(2,1)} %get-tuple-element.143), channel_id=1, source_target_pairs={{1,0},{2,1},{3,2},{4,3},{5,4},{6,5},{7,6},{8,7},{9,8},{10,9},{11,1... | collective-permute-start | bytes 221192 | tf_op jit(solution)/shard_map/ppermute | solution.py:13
  115.3 86.1 %collective-permute-start.6 = (bf16[4,3,8,384]{3,2,1,0:T(8,128)(2,1)}, bf16[4,3,8,384]{3,2,1,0:T(8,128)(2,1)S(1)}, u32[]{:S(2)}, u32[]{:S(2)}) collective-permute-start(bf16[4,3,8,384]{3,2,1,0:T(8,128)(2,1)} %get-tuple-element.142), channel_id=1, source_target_pairs={{0,1},{1,2},{2,3},{3,4},{4,5},{5,6},{6,7},{7,8},{8,9},{9,10},{10,1... | collective-permute-start | bytes 221192 | tf_op jit(solution)/shard_map/ppermute | solution.py:13
  120.9 3.1 %collective-permute-start.2 = (f32[384]{0:T(512)S(1)}, f32[384]{0:T(512)S(1)}, u32[]{:S(2)}, u32[]{:S(2)}) collective-permute-start(f32[384]{0:T(512)S(1)} %broadcast_multiply_fusion.2), channel_id=1, source_target_pairs={{0,1},{1,0},{2,3},{3,2},{4,5},{5,4},{6,7},{7,6},{8,9},{9,8},{10,11... | collective-permute-start | bytes 4616 | tf_op jit(solution)/shard_map/ppermute | solution.py:156
  123.9 3.8 %collective-permute-start.3 = (f32[384]{0:T(512)S(1)}, f32[384]{0:T(512)S(1)}, u32[]{:S(2)}, u32[]{:S(2)}) collective-permute-start(f32[384]{0:T(512)S(1)} %fusion.186), channel_id=1, source_target_pairs={{0,2},{1,3},{2,0},{3,1},{4,6},{5,7},{6,4},{7,5},{8,10},{9,11},{10,... | collective-permute-start | bytes 4616 | tf_op jit(solution)/shard_map/ppermute | solution.py:156
  127.8 9.1 %collective-permute-start.4 = (f32[384]{0:T(512)S(1)}, f32[384]{0:T(512)S(1)}, u32[]{:S(2)}, u32[]{:S(2)}) collective-permute-start(f32[384]{0:T(512)S(1)} %add.418), channel_id=1, source_target_pairs={{0,4},{1,5},{2,6},{3,7},{4,0},{5,1},{6,2},{7,3},{8,12},{9,13},{10,... | collective-permute-start | bytes 4616 | tf_op jit(solution)/shard_map/ppermute | solution.py:156
  136.9 61.8 %collective-permute-start.5 = (f32[384]{0:T(512)S(1)}, f32[384]{0:T(512)S(1)}, u32[]{:S(2)}, u32[]{:S(2)}) collective-permute-start(f32[384]{0:T(512)S(1)} %add.419), channel_id=1, source_target_pairs={{0,8},{1,9},{2,10},{3,11},{4,12},{5,13},{6,14},{7,15},{8,0},{9,1},... | collective-permute-start | bytes 4616 | tf_op jit(solution)/shard_map/ppermute | solution.py:156
  (80 other events, 355.7 us)
Sparse Core Ops, SparseCore 0:
  58.4 46.2 all-reduce.2
  109.1 63.5 reduce-scatter.1
